TPU v7x, 32 devices: a whole 2x2x4 slice. The times are simulated.
32 devices in a mesh: row: 8 (over z, x), col: 4 (over y, core).
Axes of the slice: x: 2, y: 2, z: 4, core: 2. Of those that a mesh axis runs over, the one named last changes fastest.
Arguments:
- features: bfloat16 [32768, 256], P(('col', 'row')), may hold values from -6 to 6
- adjacency: bfloat16 [256, 4, 12, 128, 128], P('row', 'col'), may hold values from 0 to 0.023925781
- block_cols: int32 [256, 4, 12], P('row', 'col'), may hold values from 0 to 63, as said below
- block_live: int32 [256, 4], P('row', 'col'), may hold values from 1 to 12, as said below
- weight: bfloat16 [256, 256], replicated, may hold values from -0.375 to 0.375
- bias: float32 [256], replicated, may hold values from -3 to 3
- upstream: bfloat16 [32768, 256], P(('row', 'col')), may hold values from -6 to 6
Outputs:
- activations: bfloat16 [32768, 256], P(('row', 'col'))
- feature_grad: bfloat16 [32768, 256], P(('col', 'row'))
- weight_grad: float32 [256, 256], replicated
- bias_grad: float32 [256], replicated
Inputs may be any that keep to these rules, and one draw needn't show every extreme that they name: `block_cols`: the live slots of one block row in one column tile name distinct column blocks of that tile. Slots k with k < block_live[i, c] are live; the other slots of block_cols and adjacency are ignored. Some entry equals 12.
All inputs are finite; a program needn't handle non-finite values.
Results may differ from a plain program's by a relative error of at most 0.014.
Values may be sent and summed in bfloat16 or wider, within the bound.
No kernel may reach another device: no remote copies, remote signals or barrier semaphores. Data moves between devices by JAX's collectives and lax.ppermute only.
A program may use at most 256 MiB of HBM per device.

v0:
```python
import jax
import jax.numpy as jnp
from jax import lax
from jax.sharding import PartitionSpec as P


def local(features, adjacency, block_cols, block_live, weight, bias, upstream):
    block_rows = adjacency.shape[0]
    block_slots = adjacency.shape[2]
    block_size = adjacency.shape[3]
    feature_width = features.shape[1]
    tile_blocks = adjacency.reshape(block_rows, block_slots, block_size, block_size)
    column_ids = block_cols.reshape(block_rows, block_slots)
    live_count = block_live.reshape(block_rows)
    live_mask = lax.broadcasted_iota(jnp.int32, (block_rows, block_slots), 1) < live_count[:, None]
    feature_panel = lax.all_gather(features, "row", axis=0, tiled=True)
    panel_blocks = feature_panel.shape[0] // block_size
    picked = feature_panel.reshape(panel_blocks, block_size, feature_width)[column_ids]
    picked = jnp.where(live_mask[:, :, None, None], picked, jnp.zeros((), jnp.bfloat16))
    partial_value = jnp.einsum(
        "ikab,ikbf->iaf", tile_blocks, picked, preferred_element_type=jnp.float32
    )
    partial_value = partial_value.reshape(block_rows * block_size, feature_width)
    aggregated = lax.psum_scatter(partial_value, "col", scatter_dimension=0, tiled=True).astype(
        jnp.bfloat16
    )
    preact = jnp.dot(aggregated, weight, preferred_element_type=jnp.float32) + bias
    sigmoid_pre = jax.nn.sigmoid(preact)
    outputs_here = (preact * sigmoid_pre).astype(jnp.bfloat16)
    derivative = sigmoid_pre * (1.0 + preact * (1.0 - sigmoid_pre))
    grad_pre = (upstream.astype(jnp.float32) * derivative).astype(jnp.bfloat16)
    weight_part = jnp.einsum("nf,ng->fg", aggregated, grad_pre, preferred_element_type=jnp.float32)
    bias_part = jnp.sum(grad_pre.astype(jnp.float32), axis=0)
    grad_agg = jnp.einsum("ng,fg->nf", grad_pre, weight, preferred_element_type=jnp.float32).astype(
        jnp.bfloat16
    )
    weight_grad, bias_grad = lax.psum((weight_part, bias_part), ("row", "col"))
    tile_grad = lax.all_gather(grad_agg, "col", axis=0, tiled=True)
    contrib = jnp.einsum(
        "ikab,iaf->ikbf",
        tile_blocks,
        tile_grad.reshape(block_rows, block_size, feature_width),
        preferred_element_type=jnp.float32,
    )
    contrib = contrib.reshape(block_rows * block_slots, block_size, feature_width)
    target_blocks = jnp.where(live_mask, column_ids, panel_blocks).reshape(-1)
    panel_sum = jnp.zeros((panel_blocks, block_size, feature_width), jnp.float32)
    panel_sum = panel_sum.at[target_blocks].add(contrib, mode="drop")
    panel_sum = panel_sum.reshape(panel_blocks * block_size, feature_width)
    feature_grad = lax.psum_scatter(
        panel_sum.astype(jnp.bfloat16), "row", scatter_dimension=0, tiled=True
    )
    return (outputs_here, feature_grad, weight_grad, bias_grad)


def solution(mesh):
    placed = (
        P(("col", "row"), None),
        P("row", "col", None, None, None),
        P("row", "col", None),
        P("row", "col"),
        P(),
        P(),
        P(("row", "col"), None),
    )
    return jax.shard_map(
        local,
        mesh=mesh,
        in_specs=placed,
        out_specs=(P(("row", "col"), None), P(("col", "row"), None), P(), P()),
        check_vma=False,
    )
```

profile of v0, /device:TPU:0, one launch (start us, length us, event | category | flops | bytes accessed | tf_op | source)
XLA Modules:
  0.0 477.4 jit_solution(3709703805803400464)
XLA Ops:
  7.2 0.0 copy-start
  7.2 0.0 all-gather.3.cloned.1.call-start
  7.2 0.7 all-gather.3.cloned.1.call-update
  7.9 0.0 reduce-scatter.3.cloned.1.call-start
  8.0 0.7 compare_select_fusion
  8.7 0.1 copy.12
  8.8 0.1 reshape.129
  8.9 0.7 iota_compare_fusion
  9.6 76.1 %all-gather.3.cloned.1.call-done = bf16[8192,256]{1,0:T(8,128)(2,1)} async-done(((bf16[1024,256]{1,0:T(8,128)(2,1)}), bf16[8192,256]{1,0:T(8,128)(2,1)}) %all-gather.3.cloned.1.call-update) | async-done | bytes 4194320 | tf_op jit(solution)/shard_map/all_gather | solution.py:16
  85.7 15.1 %gather_fusion = bf16[384,128,256]{2,1,0:T(8,128)(2,1)} fusion(bf16[64,128,256]{2,1,0:T(8,128)(2,1)} %bitcast.35, s32[1024]{0:T(1024)S(1)} %pad_clamp_fusion), kind=kCustom, calls=%fused_computation | custom fusion | bytes 50333184 | tf_op jit(solution)/shard_map/gather | solution.py:18
  100.8 0.0 copy-start.3
  100.8 0.0 copy-start.4
  100.8 16.1 %fusion = f32[32,256,128,1]{1,2,3,0:T(8,128)} fusion(bf16[32,12,128,256]{3,2,1,0:T(8,128)(2,1)} %bitcast.36, pred[32,12]{1,0:T(8,128)(4,1)S(1)} %iota_compare_fusion, bf16[32,1,12,128,128]{4,3,2,1,0:T(8,128)(2,1)} %param.8), kind=kOutput, calls=%fused_computation.2 | convolution fusion | flops 3233808384 | bytes 41943424 | tf_op jit(solution)/shard_map/ikab,ikbf->iaf/dot_general | solution.py:20
  116.9 0.0 copy-start.2
  116.9 0.0 reduce-scatter.3.cloned.1.call-update
  116.9 0.0 all-gather.5.cloned.1.call-start
  116.9 43.2 %reduce-scatter.3.cloned.1.call-done = f32[1024,256]{1,0:T(8,128)} async-done(((f32[4096,256]{1,0:T(8,128)}), f32[1024,256]{1,0:T(8,128)}) %reduce-scatter.3.cloned.1.call-update) | async-done | bytes 1048592 | tf_op jit(solution)/shard_map/reduce_scatter | solution.py:24
  160.2 0.0 copy-done
  160.2 0.0 copy-done.3
  160.2 0.0 copy-done.4
  160.2 2.7 convert_reduce_fusion
  162.9 1.1 convolution_convert_fusion
  164.0 0.0 all-gather.5.cloned.1.call-update
  164.0 0.0 all-reduce.2.cloned.1.call-start
  164.1 0.1 lt.53
  164.2 0.0 copy-done.2
  164.2 0.1 copy.13
  164.3 0.1 reshape.124
  164.4 2.3 fusion.7
  166.7 0.0 all-reduce.2.cloned.1.call-update
  166.7 0.0 reduce-scatter.5.cloned.1.call-start
  166.8 20.0 %all-gather.5.cloned.1.call-done = bf16[4096,256]{1,0:T(8,128)(2,1)} async-done(((bf16[1024,256]{1,0:T(8,128)(2,1)}), bf16[4096,256]{1,0:T(8,128)(2,1)}) %all-gather.5.cloned.1.call-update) | async-done | bytes 2097168 | tf_op jit(solution)/shard_map/all_gather | solution.py:38
  186.7 22.5 %fusion.3 = f32[32,256,12,128]{3,1,2,0:T(8,128)} fusion(bf16[32,128,256,1]{2,1,3,0:T(8,128)(2,1)} %bitcast.39, bf16[32,1,12,128,128]{4,3,2,1,0:T(8,128)(2,1)} %param.8), kind=kOutput, calls=%fused_computation.5 | convolution fusion | flops 3221225472 | bytes 65011712 | tf_op jit(solution)/shard_map/ikab,iaf->ikbf/dot_general | solution.py:39
  209.3 48.9 %copy.15 = f32[384,128,256]{2,1,0:T(8,128)} copy(f32[384,128,256]{1,2,0:T(8,128)} %bitcast.34) | data formatting | bytes 100663296 | tf_op jit(solution)/shard_map/reshape | solution.py:45
  258.2 4.2 broadcast_in_dim.23
  262.4 0.0 copy-start.1
  262.4 109.8 %scatter_fusion = f32[64,128,256]{2,1,0:T(8,128)} fusion(f32[64,128,256]{2,1,0:T(8,128)} %broadcast_in_dim.23, s32[384]{0:T(512)S(1)} %fusion.10, f32[384,128,256]{2,1,0:T(8,128)} %copy.15), kind=kCustom, calls=%fused_computation.1 | custom fusion | flops 12582912 | bytes 150996480 | tf_op jit(solution)/shard_map/scatter-add | solution.py:48
  372.2 5.9 %convert_element_type.29 = bf16[64,128,256]{2,1,0:T(8,128)(2,1)} convert(f32[64,128,256]{2,1,0:T(8,128)} %scatter_fusion) | non-fusion elementwise | flops 2097152 | bytes 12582912 | tf_op jit(solution)/shard_map/convert_element_type | solution.py:51
  378.1 0.0 reduce-scatter.5.cloned.1.call-update
  378.1 43.6 %psum.15 = f32[256]{0:T(256)} all-reduce(f32[256]{0:T(256)S(1)} %get-tuple-element.4), channel_id=1, replica_groups=mesh['row'=8,'col'=4] {'row','col'}, use_global_device_ids=true, to_apply=%region_5.6 | all-reduce | flops 256 | bytes 2048 | tf_op jit(solution)/shard_map/psum | solution.py:37
  421.8 0.0 all-reduce.2.cloned.1.call-done
  421.8 47.4 %reduce-scatter.5.cloned.1.call-done = bf16[1024,256]{1,0:T(8,128)(2,1)} async-done(((bf16[8192,256]{1,0:T(8,128)(2,1)}), bf16[1024,256]{1,0:T(8,128)(2,1)}) %reduce-scatter.5.cloned.1.call-update) | async-done | bytes 524304 | tf_op jit(solution)/shard_map/reduce_scatter | solution.py:50
  469.2 1.7 copy.22
  470.8 0.0 copy-done.1
  (2 shorter events, 0.0 us)
Async XLA Ops:
  7.2 153.0 %copy-start = (bf16[256,256]{1,0:T(8,128)(2,1)S(1)}, bf16[256,256]{1,0:T(8,128)(2,1)}, u32[]{:S(2)}) copy-start(bf16[256,256]{1,0:T(8,128)(2,1)} %param.11) | copy-start | bytes 393220
  7.2 78.5 %all-gather.3.cloned.1.call-start = ((), (), s32[]{:S(2)}) async-start(), calls=%async_computation.2 | async-start | bytes 4718592 | tf_op jit(solution)/shard_map/all_gather | solution.py:16
  7.9 152.3 %reduce-scatter.3.cloned.1.call-start = ((), (), s32[]{:S(2)}) async-start(), calls=%async_computation.3 | async-start | bytes 5242880 | tf_op jit(solution)/shard_map/reduce_scatter | solution.py:24
  100.8 59.4 %copy-start.3 = (bf16[1024,256]{1,0:T(8,128)(2,1)S(1)}, bf16[1024,256]{1,0:T(8,128)(2,1)}, u32[]{:S(2)}) copy-start(bf16[1024,256]{1,0:T(8,128)(2,1)} %param.13) | copy-start | bytes 1572868
  100.8 59.4 %copy-start.4 = (f32[256]{0:T(256)S(1)}, f32[256]{0:T(256)}, u32[]{:S(2)}) copy-start(f32[256]{0:T(256)} %param.12) | copy-start | bytes 3076
  116.9 47.3 %copy-start.2 = (s32[32,1,12]{0,1,2:T(1,128)S(1)}, s32[32,1,12]{0,1,2:T(1,128)}, u32[]{:S(2)}) copy-start(s32[32,1,12]{0,1,2:T(1,128)} %param.9) | copy-start | bytes 4612
  116.9 69.9 %all-gather.5.cloned.1.call-start = ((), (), s32[]{:S(2)}) async-start(), calls=%async_computation.4 | async-start | bytes 2621440 | tf_op jit(solution)/shard_map/all_gather | solution.py:38
  164.0 257.8 %all-reduce.2.cloned.1.call-start = ((), (), s32[]{:S(2)}) async-start(), calls=%async_computation.6 | async-start | bytes 524288 | tf_op jit(solution)/shard_map/psum | solution.py:37
  166.7 302.4 %reduce-scatter.5.cloned.1.call-start = ((), (), s32[]{:S(2)}) async-start(), calls=%async_computation.5 | async-start | bytes 4718592 | tf_op jit(solution)/shard_map/reduce_scatter | solution.py:50
  262.4 208.4 %copy-start.1 = (bf16[256,256]{1,0:T(8,128)(2,1)S(1)}, bf16[256,256]{1,0:T(8,128)(2,1)}, u32[]{:S(2)}) copy-start(bf16[256,256]{1,0:T(8,128)(2,1)} %param.11) | copy-start | bytes 393220
Sparse Core Ops, SparseCore 0:
  10.1 75.4 all-gather.2
  117.0 43.1 reduce-scatter.2
  164.2 22.5 all-gather.4
  192.7 126.5 all-reduce.1
  378.3 90.8 reduce-scatter.4
where the time goes:
time: 479 us; the launch traced here: 477 us
  waiting for transfers between devices  187 us (39%)
  other arithmetic  117 us (24%)
  local copies, waits for them, and re-layouts  70.4 us (15%)
  matrix products  44.7 us (9%)
  blocking collectives  43.6 us (9%)
  between operations  13.8 us (3%)
    scatter-add x1, other arithmetic, local(): panel_sum = panel_sum.at[target_blocks].add(contrib, mode='drop')  110 us
    all_gather x1, waiting for transfers between devices, local(): feature_panel = lax.all_gather(features, 'row', axis=0, tiled=True)  76.1 us
    reshape x1, local copies, waits for them, and re-layouts, local(): contrib.reshape(block_rows * block_slots, block_size, feature_width)  48.9 us
    reduce_scatter x1, waiting for transfers between devices, local(): lax.psum_scatter(panel_sum.astype(jnp.bfloat16), 'row', scatter_dimension...  47.4 us
    psum x1, blocking collectives, local(): weight_grad, bias_grad = lax.psum((weight_part, bias_part), ('row', 'col'))  43.6 us
    reduce_scatter x1, waiting for transfers between devices, local(): lax.psum_scatter(partial_value, 'col', scatter_dimension=0, tiled=True)  43.2 us
    dot_general x1, matrix products, local(): jnp.einsum('ikab,iaf->ikbf', tile_blocks, tile_grad.reshape(block_rows, b...  22.5 us
    all_gather x1, waiting for transfers between devices, local(): tile_grad = lax.all_gather(grad_agg, 'col', axis=0, tiled=True)  20 us
  transfers between devices with their start and end apart: 5, of which 4 were waited for; matrix products, arithmetic and copies ran while one was open for 41% of the time, Pallas kernels for 0%

commit v1 on v0

--- a/solution.py
+++ b/solution.py
@@ -2,9 +2,16 @@
 import jax.numpy as jnp
 from jax import lax
 from jax.sharding import PartitionSpec as P
+from jax.lax import psum
 
 
 def local(features, adjacency, block_cols, block_live, weight, bias, upstream):
+
+    def grid_attach(values, ax_name, row_axis):
+        for no in (ax_name, row_axis):
+            values = psum(values, no)
+        return values
+
     block_rows = adjacency.shape[0]
     block_slots = adjacency.shape[2]
     block_size = adjacency.shape[3]
@@ -34,7 +41,7 @@
     grad_agg = jnp.einsum("ng,fg->nf", grad_pre, weight, preferred_element_type=jnp.float32).astype(
         jnp.bfloat16
     )
-    weight_grad, bias_grad = lax.psum((weight_part, bias_part), ("row", "col"))
+    weight_grad, bias_grad = grid_attach((weight_part, bias_part), "col", "row")
     tile_grad = lax.all_gather(grad_agg, "col", axis=0, tiled=True)
     contrib = jnp.einsum(
         "ikab,iaf->ikbf",

time: 479 us -> 513 us (1.071)
  waiting for transfers between devices: 187 us -> 235 us
  blocking collectives: 43.6 us -> 30.7 us
    psum x1 -> x2, waiting for transfers between devices: 0.01 us -> 30.8 us  [grid_attach(): values = psum(values, no)]
    psum x1 -> x2, blocking collectives: 43.6 us -> 30.7 us  [grid_attach(): values = psum(values, no)]
    reduce_scatter x1, waiting for transfers between devices: 47.4 us -> 59.8 us  [local(): lax.psum_scatter(panel_sum.astype(jnp.bfloat16), 'row', scatter_dimension...]
  transfers between devices with their start and end apart: 5 -> 6, of which waited for: 4 -> 5; matrix products, arithmetic and copies ran while one was open for 41% -> 38% of each run, Pallas kernels for 0% -> 0%
where the time goes in v1:
time: 513 us; the launch traced here: 512 us
  waiting for transfers between devices  235 us (46%)
  other arithmetic  117 us (23%)
  local copies, waits for them, and re-layouts  70.4 us (14%)
  matrix products  44.7 us (9%)
  blocking collectives  30.7 us (6%)
  between operations  14.2 us (3%)
    scatter-add x1, other arithmetic, local(): panel_sum = panel_sum.at[target_blocks].add(contrib, mode='drop')  109 us
    all_gather x1, waiting for transfers between devices, local(): feature_panel = lax.all_gather(features, 'row', axis=0, tiled=True)  76.1 us
    reduce_scatter x1, waiting for transfers between devices, local(): lax.psum_scatter(panel_sum.astype(jnp.bfloat16), 'row', scatter_dimension...  59.8 us
    reshape x1, local copies, waits for them, and re-layouts, local(): contrib.reshape(block_rows * block_slots, block_size, feature_width)  48.9 us
    reduce_scatter x1, waiting for transfers between devices, local(): lax.psum_scatter(partial_value, 'col', scatter_dimension=0, tiled=True)  43.2 us
    psum x2, waiting for transfers between devices, grid_attach(): values = psum(values, no)  30.8 us
    psum x2, blocking collectives, grid_attach(): values = psum(values, no)  30.7 us
    all_gather x1, waiting for transfers between devices, local(): tile_grad = lax.all_gather(grad_agg, 'col', axis=0, tiled=True)  24.5 us
  transfers between devices with their start and end apart: 6, of which 5 were waited for; matrix products, arithmetic and copies ran while one was open for 38% of the time, Pallas kernels for 0%

profile of v1, /device:TPU:0, one launch (start us, length us, event | category | flops | bytes accessed | tf_op | source)
XLA Modules:
  0.0 511.9 jit_solution(1806104329781706127)
XLA Ops:
  7.2 0.0 copy-start
  7.2 0.0 all-gather.3.cloned.1.call-start
  7.2 0.7 all-gather.3.cloned.1.call-update
  7.9 0.0 reduce-scatter.3.cloned.1.call-start
  8.0 0.7 compare_select_fusion
  8.7 0.1 copy.12
  8.8 0.1 reshape.129
  8.9 0.7 iota_compare_fusion
  9.6 76.1 %all-gather.3.cloned.1.call-done = bf16[8192,256]{1,0:T(8,128)(2,1)} async-done(((bf16[1024,256]{1,0:T(8,128)(2,1)}), bf16[8192,256]{1,0:T(8,128)(2,1)}) %all-gather.3.cloned.1.call-update) | async-done | bytes 4194320 | tf_op jit(solution)/shard_map/all_gather | solution.py:23
  85.7 15.1 %gather_fusion = bf16[384,128,256]{2,1,0:T(8,128)(2,1)} fusion(bf16[64,128,256]{2,1,0:T(8,128)(2,1)} %bitcast.35, s32[1024]{0:T(1024)S(1)} %pad_clamp_fusion), kind=kCustom, calls=%fused_computation | custom fusion | bytes 50333184 | tf_op jit(solution)/shard_map/gather | solution.py:25
  100.8 0.0 copy-start.3
  100.8 0.0 copy-start.4
  100.8 16.1 %fusion = f32[32,256,128,1]{1,2,3,0:T(8,128)} fusion(bf16[32,12,128,256]{3,2,1,0:T(8,128)(2,1)} %bitcast.36, pred[32,12]{1,0:T(8,128)(4,1)S(1)} %iota_compare_fusion, bf16[32,1,12,128,128]{4,3,2,1,0:T(8,128)(2,1)} %param.8), kind=kOutput, calls=%fused_computation.2 | convolution fusion | flops 3233808384 | bytes 41943424 | tf_op jit(solution)/shard_map/ikab,ikbf->iaf/dot_general | solution.py:27
  116.9 0.0 copy-start.2
  116.9 0.0 reduce-scatter.3.cloned.1.call-update
  116.9 0.0 all-reduce.3.cloned.1.call-start
  116.9 43.2 %reduce-scatter.3.cloned.1.call-done = f32[1024,256]{1,0:T(8,128)} async-done(((f32[4096,256]{1,0:T(8,128)}), f32[1024,256]{1,0:T(8,128)}) %reduce-scatter.3.cloned.1.call-update) | async-done | bytes 1048592 | tf_op jit(solution)/shard_map/reduce_scatter | solution.py:31
  160.2 0.0 copy-done
  160.2 0.0 copy-done.3
  160.2 0.0 copy-done.4
  160.2 2.7 convert_reduce_fusion
  162.9 2.3 fusion.7
  165.1 0.0 all-reduce.3.cloned.1.call-update
  165.2 0.0 all-gather.5.cloned.1.call-start
  165.2 1.1 convolution_convert_fusion
  166.3 0.0 all-gather.5.cloned.1.call-update
  166.4 0.0 all-reduce.5.cloned.1.call-start
  166.4 0.1 lt.53
  166.5 0.0 copy-done.2
  166.5 0.1 copy.13
  166.6 0.1 reshape.124
  166.7 30.8 %all-reduce.3.cloned.1.call-done = f32[256,256]{1,0:T(8,128)} async-done(((f32[256,256]{1,0:T(8,128)}), f32[256,256]{1,0:T(8,128)}) %all-reduce.3.cloned.1.call-update) | async-done | bytes 262160 | tf_op jit(solution)/shard_map/psum | solution.py:12
  197.6 0.0 all-reduce.5.cloned.1.call-update
  197.6 0.0 reduce-scatter.5.cloned.1.call-start
  197.7 24.5 %all-gather.5.cloned.1.call-done = bf16[4096,256]{1,0:T(8,128)(2,1)} async-done(((bf16[1024,256]{1,0:T(8,128)(2,1)}), bf16[4096,256]{1,0:T(8,128)(2,1)}) %all-gather.5.cloned.1.call-update) | async-done | bytes 2097168 | tf_op jit(solution)/shard_map/all_gather | solution.py:45
  222.2 22.5 %fusion.3 = f32[32,256,12,128]{3,1,2,0:T(8,128)} fusion(bf16[32,128,256,1]{2,1,3,0:T(8,128)(2,1)} %bitcast.39, bf16[32,1,12,128,128]{4,3,2,1,0:T(8,128)(2,1)} %param.8), kind=kOutput, calls=%fused_computation.5 | convolution fusion | flops 3221225472 | bytes 65011712 | tf_op jit(solution)/shard_map/ikab,iaf->ikbf/dot_general | solution.py:46
  244.7 48.9 %copy.15 = f32[384,128,256]{2,1,0:T(8,128)} copy(f32[384,128,256]{1,2,0:T(8,128)} %bitcast.34) | data formatting | bytes 100663296 | tf_op jit(solution)/shard_map/reshape | solution.py:52
  293.5 4.2 broadcast_in_dim.23
  297.8 0.0 copy-start.1
  297.8 109.2 %scatter_fusion = f32[64,128,256]{2,1,0:T(8,128)} fusion(f32[64,128,256]{2,1,0:T(8,128)} %broadcast_in_dim.23, s32[384]{0:T(512)S(1)} %fusion.10, f32[384,128,256]{2,1,0:T(8,128)} %copy.15), kind=kCustom, calls=%fused_computation.1 | custom fusion | flops 12582912 | bytes 150996480 | tf_op jit(solution)/shard_map/scatter-add | solution.py:55
  407.0 5.9 %convert_element_type.29 = bf16[64,128,256]{2,1,0:T(8,128)(2,1)} convert(f32[64,128,256]{2,1,0:T(8,128)} %scatter_fusion) | non-fusion elementwise | flops 2097152 | bytes 12582912 | tf_op jit(solution)/shard_map/convert_element_type | solution.py:58
  412.9 0.0 reduce-scatter.5.cloned.1.call-update
  412.9 7.0 %psum.30 = f32[256]{0:T(256)S(1)} all-reduce(f32[256]{0:T(256)S(1)} %get-tuple-element.4), channel_id=1, replica_groups=mesh['row'=8,'col'=4] {'col'}, use_global_device_ids=true, to_apply=%region_6.7 | all-reduce | flops 256 | bytes 2048 | tf_op jit(solution)/shard_map/psum | solution.py:12
  420.0 23.6 %psum.31 = f32[256]{0:T(256)} all-reduce(f32[256]{0:T(256)S(1)} %psum.30), channel_id=1, replica_groups=mesh['row'=8,'col'=4] {'row'}, use_global_device_ids=true, to_apply=%region_7.8 | all-reduce | flops 256 | bytes 2048 | tf_op jit(solution)/shard_map/psum | solution.py:12
  443.6 0.0 all-reduce.5.cloned.1.call-done
  443.6 59.8 %reduce-scatter.5.cloned.1.call-done = bf16[1024,256]{1,0:T(8,128)(2,1)} async-done(((bf16[8192,256]{1,0:T(8,128)(2,1)}), bf16[1024,256]{1,0:T(8,128)(2,1)}) %reduce-scatter.5.cloned.1.call-update) | async-done | bytes 524304 | tf_op jit(solution)/shard_map/reduce_scatter | solution.py:57
  503.4 1.7 copy.23
  505.1 0.0 copy-done.1
  (2 shorter events, 0.0 us)
Async XLA Ops:
  7.2 153.0 %copy-start = (bf16[256,256]{1,0:T(8,128)(2,1)S(1)}, bf16[256,256]{1,0:T(8,128)(2,1)}, u32[]{:S(2)}) copy-start(bf16[256,256]{1,0:T(8,128)(2,1)} %param.11) | copy-start | bytes 393220
  7.2 78.5 %all-gather.3.cloned.1.call-start = ((), (), s32[]{:S(2)}) async-start(), calls=%async_computation.2 | async-start | bytes 4718592 | tf_op jit(solution)/shard_map/all_gather | solution.py:23
  7.9 152.2 %reduce-scatter.3.cloned.1.call-start = ((), (), s32[]{:S(2)}) async-start(), calls=%async_computation.3 | async-start | bytes 5242880 | tf_op jit(solution)/shard_map/reduce_scatter | solution.py:31
  100.8 59.4 %copy-start.3 = (bf16[1024,256]{1,0:T(8,128)(2,1)S(1)}, bf16[1024,256]{1,0:T(8,128)(2,1)}, u32[]{:S(2)}) copy-start(bf16[1024,256]{1,0:T(8,128)(2,1)} %param.13) | copy-start | bytes 1572868
  100.8 59.4 %copy-start.4 = (f32[256]{0:T(256)S(1)}, f32[256]{0:T(256)}, u32[]{:S(2)}) copy-start(f32[256]{0:T(256)} %param.12) | copy-start | bytes 3076
  116.9 49.7 %copy-start.2 = (s32[32,1,12]{0,1,2:T(1,128)S(1)}, s32[32,1,12]{0,1,2:T(1,128)}, u32[]{:S(2)}) copy-start(s32[32,1,12]{0,1,2:T(1,128)} %param.9) | copy-start | bytes 4612
  116.9 80.7 %all-reduce.3.cloned.1.call-start = ((), (), s32[]{:S(2)}) async-start(), calls=%async_computation.6 | async-start | bytes 524288 | tf_op jit(solution)/shard_map/psum | solution.py:12
  165.2 57.0 %all-gather.5.cloned.1.call-start = ((), (), s32[]{:S(2)}) async-start(), calls=%async_computation.4 | async-start | bytes 2621440 | tf_op jit(solution)/shard_map/all_gather | solution.py:45
  166.4 277.3 %all-reduce.5.cloned.1.call-start = ((), (), s32[]{:S(2)}) async-start(), calls=%async_computation.7 | async-start | bytes 524288 | tf_op jit(solution)/shard_map/psum | solution.py:12
  197.6 305.8 %reduce-scatter.5.cloned.1.call-start = ((), (), s32[]{:S(2)}) async-start(), calls=%async_computation.5 | async-start | bytes 4718592 | tf_op jit(solution)/shard_map/reduce_scatter | solution.py:57
  297.8 207.3 %copy-start.1 = (bf16[256,256]{1,0:T(8,128)(2,1)S(1)}, bf16[256,256]{1,0:T(8,128)(2,1)}, u32[]{:S(2)}) copy-start(bf16[256,256]{1,0:T(8,128)(2,1)} %param.11) | copy-start | bytes 393220
Sparse Core Ops, SparseCore 0:
  10.1 75.4 all-gather.2
  117.0 43.1 reduce-scatter.2
  165.3 32.2 all-reduce.2
  199.6 22.5 all-gather.4
  225.4 71.0 all-reduce.4
  413.1 90.3 reduce-scatter.4
